TPU v7x, 256 devices: a whole 4x4x8 slice. The times are simulated.
256 devices in a mesh: ctx: 8 (over z_lo, y), exp: 32 (over z_hi, x, core).
Axes of the slice: x: 4, y: 4, z: 8 (z_hi: 4, z_lo: 2; z = z_hi * 2 + z_lo), core: 2. Of those that a mesh axis runs over, the one named last changes fastest.
Arguments:
- tokens: bfloat16 [32, 1024, 2048], P('exp', 'ctx'), may hold values from -6 to 6
- queries: bfloat16 [32, 1024, 1024], P('exp', 'ctx'), may hold values from -60 to 60
- keys: bfloat16 [32, 1024, 1024], P('exp', 'ctx'), may hold values from -4 to 4
- values: bfloat16 [32, 1024, 1024], P('exp', 'ctx'), may hold values from -12 to 12
- out_proj: bfloat16 [1024, 2048], replicated, may hold values from -0.1875 to 0.1875
- mod_scale: float32 [32, 2048], P('exp'), may hold values from -2.5 to 2.5
- mod_shift: float32 [32, 2048], P('exp'), may hold values from -2.5 to 2.5
- expert_ids: int32 [32, 1024, 2], P('exp', 'ctx'), may hold values from 0 to 63, all different within a row; in each aligned block of 128 rows (0 to 127, 128 to 255, ..., all dimensions but the last counted through in order) at most 6 rows name the same one
- gates: float32 [32, 1024, 2], P('exp', 'ctx'), may hold values from 0.2 to 1
- w_gate: bfloat16 [65536, 2048], P(('ctx', 'exp')), may hold values from -0.125 to 0.125
- w_up: bfloat16 [65536, 2048], P(('ctx', 'exp')), may hold values from -0.125 to 0.125
- w_down: bfloat16 [65536, 2048], P(('ctx', 'exp')), may hold values from -0.1875 to 0.1875
- out_grad: bfloat16 [32, 1024, 2048], P('exp', 'ctx'), may hold values from -0.1875 to 0.1875
Outputs:
- layer_out: bfloat16 [32, 1024, 2048], P('exp', 'ctx')
- grad_gate: bfloat16 [65536, 2048], P(('ctx', 'exp'))
- grad_up: bfloat16 [65536, 2048], P(('ctx', 'exp'))
- grad_down: bfloat16 [65536, 2048], P(('ctx', 'exp'))
Inputs may be any that keep to these rules, and one draw needn't show every extreme that they name: `expert_ids`: the two ids of a token differ. Among the 128 tokens of one device no expert is named more than 6 times, and in some device some expert exactly 6 times.
All inputs are finite; a program needn't handle non-finite values.
Results may differ from a plain program's by a relative error of at most 0.0075.
Values may be sent and summed in bfloat16 or wider, within the bound.
A program may use at most 128 MiB of HBM per device.

v0:
```python
import jax
import jax.numpy as jnp
from jax import lax
from jax.sharding import PartitionSpec as P

HEADS = 8
HD = 128
SHARDS = 4


def per_device(
    tokens,
    queries,
    keys,
    values,
    out_proj,
    mod_scale,
    mod_shift,
    expert_ids,
    gates,
    w_gate,
    w_up,
    w_down,
    out_grad,
):
    ctx_count = lax.axis_size("ctx")
    exp_count = lax.axis_size("exp")
    local_tokens = tokens.shape[1]
    model_width = tokens.shape[2]
    score_scale = HD ** (-0.5)
    query_rows = queries[0]
    key_rows = keys[0]
    value_rows = values[0]
    query_heads = query_rows.reshape(local_tokens, HEADS, HD)
    running_top = jnp.full((HEADS, local_tokens), -1e30, jnp.float32)
    key_piece = lax.all_gather(key_rows, "ctx", axis=0, tiled=True).reshape(-1, HEADS, HD)
    value_piece = lax.all_gather(value_rows, "ctx", axis=0, tiled=True).reshape(-1, HEADS, HD)
    scores = (
        jnp.einsum("qhd,khd->hqk", query_heads, key_piece, preferred_element_type=jnp.float32)
        * score_scale
    )
    new_top = jnp.maximum(running_top, jnp.max(scores, axis=-1))
    exponent = jnp.exp(scores - new_top[..., None])
    running_sum = jnp.sum(exponent, axis=-1)
    accum = jnp.einsum(
        "hqk,khd->hqd",
        exponent.astype(jnp.bfloat16),
        value_piece,
        preferred_element_type=jnp.float32,
    )
    attended = (
        jnp.transpose(accum / running_sum[..., None], (1, 0, 2))
        .reshape(local_tokens, HEADS * HD)
        .astype(jnp.bfloat16)
    )
    mixed = tokens[0].astype(jnp.float32) + jnp.dot(
        attended, out_proj, preferred_element_type=jnp.float32
    )
    mean_square = jnp.mean(mixed * mixed, axis=-1, keepdims=True)
    normed = (mixed * lax.rsqrt(mean_square + 1e-06) * (1.0 + mod_scale) + mod_shift).astype(
        jnp.bfloat16
    )
    expert_total = ctx_count * exp_count // SHARDS
    capacity = 3 * local_tokens // expert_total
    group_count = exp_count // SHARDS
    chosen = expert_ids[0].reshape(-1)
    one_hot = (chosen[:, None] == jnp.arange(expert_total, dtype=jnp.int32)[None, :]).astype(
        jnp.int32
    )
    before = jnp.cumsum(one_hot, axis=0) - one_hot
    slot_index = jnp.sum(one_hot * before, axis=1)
    position = chosen * capacity + slot_index
    chooser = (
        jnp.arange(expert_total * capacity, dtype=jnp.int32)[:, None] == position[None, :]
    ).astype(jnp.bfloat16)
    gate_flat = gates[0].reshape(-1)
    token_rows = jnp.repeat(normed, 2, axis=0)
    grad_rows = (
        gate_flat[:, None] * jnp.repeat(out_grad[0], 2, axis=0).astype(jnp.float32)
    ).astype(jnp.bfloat16)
    stacked = jnp.concatenate([token_rows, grad_rows], axis=1)
    placed = jnp.dot(chooser, stacked, preferred_element_type=jnp.float32).astype(jnp.bfloat16)
    slot_width = capacity * 2 * model_width
    plain_slots = placed.reshape(ctx_count, group_count, slot_width)
    middle = lax.all_to_all(plain_slots, "ctx", split_axis=0, concat_axis=0, tiled=True)
    shaped = middle.reshape(ctx_count, group_count, 1, slot_width)
    widened = jnp.broadcast_to(shaped, (ctx_count, group_count, SHARDS, slot_width))
    arrived = lax.all_to_all(
        widened.reshape(ctx_count, exp_count, slot_width),
        "exp",
        split_axis=1,
        concat_axis=1,
        tiled=True,
    )
    arrived = arrived.reshape(-1, 2 * model_width)
    expert_rows = arrived[:, :model_width]
    row_grads = arrived[:, model_width:]
    gate_pre = jnp.einsum("rd,fd->rf", expert_rows, w_gate, preferred_element_type=jnp.float32)
    up_pre = jnp.einsum("rd,fd->rf", expert_rows, w_up, preferred_element_type=jnp.float32)
    sigmoid_gate = jax.nn.sigmoid(gate_pre)
    activation = gate_pre * sigmoid_gate
    hidden = (activation * up_pre).astype(jnp.bfloat16)
    piece_out = jnp.einsum("rf,fd->rd", hidden, w_down, preferred_element_type=jnp.float32).astype(
        jnp.bfloat16
    )
    out_width = capacity * model_width
    piece_out = piece_out.reshape(ctx_count, exp_count, out_width)
    by_piece = lax.all_to_all(piece_out, "exp", split_axis=1, concat_axis=1, tiled=True)
    piece_sums = jnp.sum(
        by_piece.astype(jnp.float32).reshape(ctx_count, group_count, SHARDS, out_width), axis=2
    )
    expert_sums = lax.all_to_all(
        piece_sums.astype(jnp.bfloat16), "ctx", split_axis=0, concat_axis=0, tiled=True
    ).astype(piece_sums.dtype)
    expert_sums = expert_sums.reshape(expert_total * capacity, model_width)
    hidden_grad = jnp.einsum("rd,fd->rf", row_grads, w_down, preferred_element_type=jnp.float32)
    gate_cot = (
        hidden_grad * up_pre * sigmoid_gate * (1.0 + gate_pre * (1.0 - sigmoid_gate))
    ).astype(jnp.bfloat16)
    up_cot = (hidden_grad * activation).astype(jnp.bfloat16)
    grad_down = jnp.einsum(
        "rf,rd->fd", hidden, row_grads, preferred_element_type=jnp.float32
    ).astype(jnp.bfloat16)
    grad_gate = jnp.einsum(
        "rf,rd->fd", gate_cot, expert_rows, preferred_element_type=jnp.float32
    ).astype(jnp.bfloat16)
    grad_up = jnp.einsum(
        "rf,rd->fd", up_cot, expert_rows, preferred_element_type=jnp.float32
    ).astype(jnp.bfloat16)
    picked = jnp.take(expert_sums, position, axis=0)
    combined = jnp.sum((gate_flat[:, None] * picked).reshape(local_tokens, 2, model_width), axis=1)
    layer_out = (mixed + combined).astype(jnp.bfloat16)[None]
    return (layer_out, grad_gate, grad_up, grad_down)


def solution(mesh):
    placed = (
        P("exp", "ctx", None),
        P("exp", "ctx", None),
        P("exp", "ctx", None),
        P("exp", "ctx", None),
        P(),
        P("exp", None),
        P("exp", None),
        P("exp", "ctx", None),
        P("exp", "ctx", None),
        P(("ctx", "exp"), None),
        P(("ctx", "exp"), None),
        P(("ctx", "exp"), None),
        P("exp", "ctx", None),
    )
    return jax.shard_map(
        per_device,
        mesh=mesh,
        in_specs=placed,
        out_specs=(
            P("exp", "ctx", None),
            P(("ctx", "exp"), None),
            P(("ctx", "exp"), None),
            P(("ctx", "exp"), None),
        ),
        check_vma=False,
    )
```

profile of v0, /device:TPU:3, one launch (start us, length us, event | category | flops | bytes accessed | tf_op | source)
XLA Modules:
  0.0 742.8 jit_solution(3102636036667470510)
XLA Ops:
  7.2 1.9 copy.84
  9.2 0.7 all-gather.7.cloned.1.call-update
  9.9 0.8 copy.89
  11.0 1.0 copy.102
  13.5 2.5 broadcast_in_dim.36
  16.0 2.7 convert_element_type.81
  18.9 0.7 mul.118
  19.6 0.8 fusion.48
  20.4 1.8 multiply_convert_fusion
  22.2 34.2 %all-gather.5.cloned.1.call-done = bf16[1,1024,1024]{1,2,0:T(8,128)(2,1)} async-done(((bf16[1,128,1024]{1,2,0:T(8,128)(2,1)}), bf16[1,1024,1024]{1,2,0:T(8,128)(2,1)}) %all-gather.5.cloned.1.call-update) | async-done | bytes 2097168 | tf_op jit(solution)/shard_map/all_gather | solution.py:36
  56.5 2.4 multiply_reduce_fusion
  58.9 1.9 copy-done.1
  60.8 0.9 fusion.12
  61.7 40.5 %all-gather.7.cloned.1.call-done = bf16[1,1024,1024]{2,1,0:T(8,128)(2,1)} async-done(((bf16[1,128,1024]{2,1,0:T(8,128)(2,1)}), bf16[1,1024,1024]{2,1,0:T(8,128)(2,1)}) %all-gather.7.cloned.1.call-update) | async-done | bytes 2097168 | tf_op jit(solution)/shard_map/all_gather | solution.py:37
  102.2 2.9 copy.87
  105.1 3.4 fusion.37
  108.7 0.8 multiply_reduce_fusion.2
  109.7 0.6 broadcast_in_dim.35
  110.4 1.2 reshape.142
  111.6 4.2 convolution_convert_fusion.1
  115.7 6.3 reshape.143
  122.0 35.0 %all_to_all.20 = bf16[8,8,24576]{2,1,0:T(8,128)(2,1)S(1)} all-to-all(bf16[8,8,24576]{2,1,0:T(8,128)(2,1)} %reshape.143), channel_id=1, replica_groups=mesh['ctx'=8,'exp'=32] {'ctx'}, dimensions={0} | all-to-all | bytes 6291456 | tf_op jit(solution)/shard_map/all_to_all | solution.py:85
  157.0 3.4 copy.95
  160.4 8.0 %broadcast_in_dim.37 = bf16[8,8,4,24576]{3,0,2,1:T(8,128)(2,1)} broadcast(bf16[8,8,24576]{2,0,1:T(8,128)(2,1)} %copy.95), dimensions={0,1,3} | broadcast | bytes 15728640 | tf_op jit(solution)/shard_map/broadcast_in_dim | solution.py:87
  168.4 291.2 %all_to_all.21 = bf16[8,32,24576]{2,0,1:T(8,128)(2,1)S(1)} all-to-all(bf16[8,32,24576]{2,0,1:T(8,128)(2,1)} %bitcast.62), channel_id=1, replica_groups=mesh['ctx'=8,'exp'=32] {'exp'}, dimensions={1} | all-to-all | bytes 25165824 | tf_op jit(solution)/shard_map/all_to_all | solution.py:88
  459.6 19.8 %copy.96 = bf16[8,32,24576]{2,1,0:T(8,128)(2,1)} copy(bf16[8,32,24576]{2,0,1:T(8,128)(2,1)S(1)} %all_to_all.21) | data formatting | bytes 25165824 | tf_op jit(solution)/shard_map/all_to_all | solution.py:88
  479.5 20.7 %reshape.145 = bf16[1536,4096]{1,0:T(8,128)(2,1)} reshape(bf16[8,32,24576]{2,1,0:T(8,128)(2,1)} %copy.96) | data formatting | bytes 25165824 | tf_op jit(solution)/shard_map/reshape | solution.py:95
  500.2 4.9 fusion.10
  505.0 1.5 copy-done.2
  506.8 3.4 multiply_convert_fusion.3
  510.2 4.4 convolution_convert_fusion
  514.6 12.5 %reshape.146 = bf16[8,32,12288]{2,1,0:T(8,128)(2,1)} reshape(bf16[1536,2048]{1,0:T(8,128)(2,1)} %convolution_convert_fusion) | data formatting | bytes 12582912 | tf_op jit(solution)/shard_map/reshape | solution.py:107
  527.1 8.8 %copy.97 = bf16[8,32,12288]{2,0,1:T(8,128)(2,1)} copy(bf16[8,32,12288]{2,1,0:T(8,128)(2,1)} %reshape.146) | data formatting | bytes 12582912 | tf_op jit(solution)/shard_map/reshape | solution.py:107
  536.0 7.2 all-to-all-start.2
  544.0 141.3 %all-to-all-done.2 = bf16[8,32,12288]{2,0,1:T(8,128)(2,1)} async-done(((bf16[8,32,12288]{2,0,1:T(8,128)(2,1)}), bf16[8,32,12288]{2,0,1:T(8,128)(2,1)}, u32[]{:S(2)}, u32[]{:S(2)}) %all-to-all-start.2) | async-done | bytes 6291488 | tf_op jit(solution)/shard_map/all_to_all | solution.py:108
  685.3 3.7 bitcast_reduce_fusion
  689.0 2.0 copy.98
  691.0 4.3 all-to-all-start.3
  695.3 5.7 fusion.20
  701.1 4.9 fusion.2
  706.0 2.9 fusion.17
  708.9 3.2 fusion.14
  712.0 3.5 all-to-all-done.3
  715.6 4.4 reshape.154
  719.9 5.5 gather_fusion
  725.5 3.5 gather.7
  729.0 5.7 multiply_reduce_fusion.1
  734.6 0.9 fusion.41
  (62 shorter events, 3.4 us)
Async XLA Ops:
  7.2 503.0 %copy-start = (bf16[256,2048]{1,0:T(8,128)(2,1)S(1)}, bf16[256,2048]{1,0:T(8,128)(2,1)}, u32[]{:S(2)}) copy-start(bf16[256,2048]{1,0:T(8,128)(2,1)} %param.24) | copy-start | bytes 3145732
  7.2 6.2 copy-start.4
  7.2 49.3 %all-gather.5.cloned.1.call-start = ((), (), s32[]{:S(2)}) async-start(), calls=%async_computation.4 | async-start | bytes 2359296 | tf_op jit(solution)/shard_map/all_gather | solution.py:36
  9.2 93.1 %all-gather.7.cloned.1.call-start = ((), (), s32[]{:S(2)}) async-start(), calls=%async_computation.5 | async-start | bytes 2359296 | tf_op jit(solution)/shard_map/all_gather | solution.py:37
  16.0 2.7 copy-start.9
  16.0 4.3 copy-start.8
  58.8 1.9 copy-start.1
  105.1 3.5 copy-start.3
  105.1 3.6 copy-start.5
  108.7 0.8 copy-start.7
  479.5 20.7 %copy-start.10 = (bf16[256,2048]{1,0:T(8,128)(2,1)S(1)}, bf16[256,2048]{1,0:T(8,128)(2,1)}, u32[]{:S(2)}) copy-start(bf16[256,2048]{1,0:T(8,128)(2,1)} %param.22) | copy-start | bytes 3145732
  500.2 6.4 copy-start.2
  500.2 6.6 copy-start.11
  506.8 3.4 copy-start.12
  536.0 7.4 copy-start.6
  536.0 149.3 %all-to-all-start.2 = ((bf16[8,32,12288]{2,0,1:T(8,128)(2,1)}), bf16[8,32,12288]{2,0,1:T(8,128)(2,1)}, u32[]{:S(2)}, u32[]{:S(2)}) async-start(bf16[8,32,12288]{2,0,1:T(8,128)(2,1)} %copy.97), calls=%async_computation.2 | async-start | bytes 12582912 | tf_op jit(solution)/shard_map/all_to_all | solution.py:108
  691.0 24.6 %all-to-all-start.3 = ((bf16[8,8,12288]{2,1,0:T(8,128)(2,1)}), bf16[8,8,12288]{2,1,0:T(8,128)(2,1)}, u32[]{:S(2)}, u32[]{:S(2)}) async-start(bf16[8,8,12288]{2,1,0:T(8,128)(2,1)} %copy.98), calls=%async_computation.3 | async-start | bytes 3145728 | tf_op jit(solution)/shard_map/all_to_all | solution.py:112
  695.3 10.6 %slice-start = ((s8[12582912]{0:T(1024)(128)(4,1)}), s8[4194304]{0:T(1024)(128)(4,1)S(1)}, s32[]{:S(2)}) async-start(s8[12582912]{0:T(1024)(128)(4,1)} %bitcast.63), calls=%async_computation.6 | async-start | bytes 8388608
  695.3 10.6 %slice-start.1 = ((s8[12582912]{0:T(1024)(128)(4,1)}), s8[4194304]{0:T(1024)(128)(4,1)S(1)}, s32[]{:S(2)}) async-start(s8[12582912]{0:T(1024)(128)(4,1)} %bitcast.63), calls=%async_computation.7 | async-start | bytes 8388608
  701.1 4.9 slice-start.2
  701.1 4.9 copy-start.13
  706.0 2.9 copy-start.14
Sparse Core Ops, SparseCore 0:
  10.3 46.1 all-gather.4
  58.3 43.9 all-gather.6
where the time goes:
time: 751 us; the launch traced here: 743 us
  blocking collectives  326 us (43%)
  waiting for transfers between devices  220 us (29%)
  local copies, waits for them, and re-layouts  115 us (15%)
  matrix products  40 us (5%)
  other arithmetic  14.9 us (2%)
  between operations  14.8 us (2%)
  starting transfers between devices  11.6 us (2%)
    all_to_all x1, blocking collectives, per_device(): lax.all_to_all(widened.reshape(ctx_count, exp_count, slot_width), 'exp',...  291 us
    all_to_all x1, waiting for transfers between devices, per_device(): lax.all_to_all(piece_out, 'exp', split_axis=1, concat_axis=1, tiled=True)  141 us
    all_gather x1, waiting for transfers between devices, per_device(): lax.all_gather(value_rows, 'ctx', axis=0, tiled=True).reshape(-1, HEADS, HD)  40.5 us
    all_to_all x1, blocking collectives, per_device(): lax.all_to_all(plain_slots, 'ctx', split_axis=0, concat_axis=0, tiled=True)  35 us
    all_gather x1, waiting for transfers between devices, per_device(): lax.all_gather(key_rows, 'ctx', axis=0, tiled=True).reshape(-1, HEADS, HD)  34.2 us
    reshape x2, local copies, waits for them, and re-layouts, per_device(): piece_out = piece_out.reshape(ctx_count, exp_count, out_width)  21.4 us
    reshape x1, local copies, waits for them, and re-layouts, per_device(): arrived = arrived.reshape(-1, 2 * model_width)  20.7 us
    all_to_all x1, local copies, waits for them, and re-layouts, per_device(): lax.all_to_all(widened.reshape(ctx_count, exp_count, slot_width), 'exp',...  19.8 us
  transfers between devices with their start and end apart: 4, of which 4 were waited for; matrix products, arithmetic and copies ran while one was open for 4% of the time, Pallas kernels for 0%

commit v1 on v0

--- a/solution.py
+++ b/solution.py
@@ -33,7 +33,9 @@
     value_rows = values[0]
     query_heads = query_rows.reshape(local_tokens, HEADS, HD)
     running_top = jnp.full((HEADS, local_tokens), -1e30, jnp.float32)
-    key_piece = lax.all_gather(key_rows, "ctx", axis=0, tiled=True).reshape(-1, HEADS, HD)
+    key_piece = jnp.concatenate(
+        lax.all_to_all(jnp.stack([key_rows] * lax.axis_size("ctx")), "ctx", 0, 0), axis=0
+    ).reshape(-1, HEADS, HD)
     value_piece = lax.all_gather(value_rows, "ctx", axis=0, tiled=True).reshape(-1, HEADS, HD)
     scores = (
         jnp.einsum("qhd,khd->hqk", query_heads, key_piece, preferred_element_type=jnp.float32)

time: 751 us -> 716 us (0.953)
  waiting for transfers between devices: 220 us -> 173 us
    all_gather x1 -> x0, waiting for transfers between devices: 34.2 us -> none  [per_device(): lax.all_gather(key_rows, 'ctx', axis=0, tiled=True).reshape(-1, HEADS, HD)]
    all_gather x1, waiting for transfers between devices: 40.5 us -> 13 us  [per_device(): lax.all_gather(value_rows, 'ctx', axis=0, tiled=True).reshape(-1, HEADS, HD)]
    all_to_all x0 -> x1, waiting for transfers between devices: none -> 15.7 us  [per_device(): lax.all_to_all(jnp.stack([key_rows] * lax.axis_size('ctx')), 'ctx', 0, 0)]
  transfers between devices with their start and end apart: 4 -> 4, of which waited for: 4 -> 4; matrix products, arithmetic and copies ran while one was open for 4% -> 5% of each run, Pallas kernels for 0% -> 0%
where the time goes in v1:
time: 716 us; the launch traced here: 706 us
  blocking collectives  329 us (46%)
  waiting for transfers between devices  173 us (24%)
  local copies, waits for them, and re-layouts  117 us (16%)
  matrix products  38.5 us (5%)
  starting transfers between devices  17.2 us (2%)
  other arithmetic  16.8 us (2%)
  between operations  14.8 us (2%)
    all_to_all x1, blocking collectives, per_device(): lax.all_to_all(widened.reshape(ctx_count, exp_count, slot_width), 'exp',...  289 us
    all_to_all x1, waiting for transfers between devices, per_device(): lax.all_to_all(piece_out, 'exp', split_axis=1, concat_axis=1, tiled=True)  140 us
    all_to_all x1, blocking collectives, per_device(): lax.all_to_all(plain_slots, 'ctx', split_axis=0, concat_axis=0, tiled=True)  39.6 us
    reshape x2, local copies, waits for them, and re-layouts, per_device(): piece_out = piece_out.reshape(ctx_count, exp_count, out_width)  21.4 us
    reshape x1, local copies, waits for them, and re-layouts, per_device(): arrived = arrived.reshape(-1, 2 * model_width)  20.7 us
    all_to_all x1, local copies, waits for them, and re-layouts, per_device(): lax.all_to_all(widened.reshape(ctx_count, exp_count, slot_width), 'exp',...  19.9 us
    all_to_all x1, waiting for transfers between devices, per_device(): lax.all_to_all(jnp.stack([key_rows] * lax.axis_size('ctx')), 'ctx', 0, 0)  15.7 us
  transfers between devices with their start and end apart: 4, of which 4 were waited for; matrix products, arithmetic and copies ran while one was open for 5% of the time, Pallas kernels for 0%

profile of v1, /device:TPU:3, one launch (start us, length us, event | category | flops | bytes accessed | tf_op | source)
XLA Modules:
  0.0 706.4 jit_solution(16591076374008990344)
XLA Ops:
  7.2 2.6 stack.3
  9.8 5.7 all-to-all-start
  16.6 1.0 copy.95
  19.1 1.1 bitcast_convert_fusion
  20.2 2.5 broadcast_in_dim.36
  22.7 3.7 convert_element_type.81
  26.4 0.8 copy.88
  27.2 0.7 mul.118
  27.9 0.8 fusion.49
  28.7 2.7 multiply_convert_fusion
  31.5 15.7 %all-to-all-done = bf16[8,128,1024]{2,1,0:T(8,128)(2,1)S(1)} async-done(((bf16[8,128,1024]{2,1,0:T(8,128)(2,1)}), bf16[8,128,1024]{2,1,0:T(8,128)(2,1)S(1)}, u32[]{:S(2)}, u32[]{:S(2)}) %all-to-all-start) | async-done | bytes 2097184 | tf_op jit(solution)/shard_map/all_to_all | solution.py:37
  47.8 0.9 multiply_reduce_fusion
  48.7 1.9 copy-done.1
  50.6 0.9 fusion.12
  51.5 13.0 %all-gather.3.cloned.1.call-done = bf16[1,1024,1024]{2,1,0:T(8,128)(2,1)} async-done(((bf16[1,128,1024]{2,1,0:T(8,128)(2,1)}), bf16[1,1024,1024]{2,1,0:T(8,128)(2,1)}) %all-gather.3.cloned.1.call-update) | async-done | bytes 2097168 | tf_op jit(solution)/shard_map/all_gather | solution.py:39
  64.5 2.9 copy.81
  67.4 3.4 fusion.39
  71.0 0.8 multiply_reduce_fusion.2
  72.7 1.2 reshape.139
  73.9 4.2 convolution_convert_fusion.1
  78.1 6.3 reshape.140
  84.3 39.6 %all_to_all.25 = bf16[8,8,24576]{2,1,0:T(8,128)(2,1)S(1)} all-to-all(bf16[8,8,24576]{2,1,0:T(8,128)(2,1)} %reshape.140), channel_id=1, replica_groups=mesh['ctx'=8,'exp'=32] {'ctx'}, dimensions={0} | all-to-all | bytes 6291456 | tf_op jit(solution)/shard_map/all_to_all | solution.py:87
  123.9 3.4 copy.89
  127.3 8.0 %broadcast_in_dim.37 = bf16[8,8,4,24576]{3,0,2,1:T(8,128)(2,1)} broadcast(bf16[8,8,24576]{2,0,1:T(8,128)(2,1)} %copy.89), dimensions={0,1,3} | broadcast | bytes 15728640 | tf_op jit(solution)/shard_map/broadcast_in_dim | solution.py:89
  135.3 289.1 %all_to_all.26 = bf16[8,32,24576]{2,0,1:T(8,128)(2,1)S(1)} all-to-all(bf16[8,32,24576]{2,0,1:T(8,128)(2,1)} %bitcast.64), channel_id=1, replica_groups=mesh['ctx'=8,'exp'=32] {'exp'}, dimensions={1} | all-to-all | bytes 25165824 | tf_op jit(solution)/shard_map/all_to_all | solution.py:90
  424.4 19.9 %copy.90 = bf16[8,32,24576]{2,1,0:T(8,128)(2,1)} copy(bf16[8,32,24576]{2,0,1:T(8,128)(2,1)S(1)} %all_to_all.26) | data formatting | bytes 25165824 | tf_op jit(solution)/shard_map/all_to_all | solution.py:90
  444.3 20.7 %reshape.142 = bf16[1536,4096]{1,0:T(8,128)(2,1)} reshape(bf16[8,32,24576]{2,1,0:T(8,128)(2,1)} %copy.90) | data formatting | bytes 25165824 | tf_op jit(solution)/shard_map/reshape | solution.py:97
  465.0 4.9 fusion.10
  469.9 1.5 copy-done.2
  471.6 3.4 multiply_convert_fusion.3
  475.0 4.4 convolution_convert_fusion
  479.4 12.5 %reshape.143 = bf16[8,32,12288]{2,1,0:T(8,128)(2,1)} reshape(bf16[1536,2048]{1,0:T(8,128)(2,1)} %convolution_convert_fusion) | data formatting | bytes 12582912 | tf_op jit(solution)/shard_map/reshape | solution.py:109
  491.9 8.8 %copy.91 = bf16[8,32,12288]{2,0,1:T(8,128)(2,1)} copy(bf16[8,32,12288]{2,1,0:T(8,128)(2,1)} %reshape.143) | data formatting | bytes 12582912 | tf_op jit(solution)/shard_map/reshape | solution.py:109
  500.8 7.2 %all-to-all-start.3 = ((bf16[8,32,12288]{2,0,1:T(8,128)(2,1)}), bf16[8,32,12288]{2,0,1:T(8,128)(2,1)}, u32[]{:S(2)}, u32[]{:S(2)}) async-start(bf16[8,32,12288]{2,0,1:T(8,128)(2,1)} %copy.91), calls=%async_computation.3 | async-start | bytes 12582912 | tf_op jit(solution)/shard_map/all_to_all | solution.py:110
  508.8 139.7 %all-to-all-done.3 = bf16[8,32,12288]{2,0,1:T(8,128)(2,1)} async-done(((bf16[8,32,12288]{2,0,1:T(8,128)(2,1)}), bf16[8,32,12288]{2,0,1:T(8,128)(2,1)}, u32[]{:S(2)}, u32[]{:S(2)}) %all-to-all-start.3) | async-done | bytes 6291488 | tf_op jit(solution)/shard_map/all_to_all | solution.py:110
  648.5 3.7 bitcast_reduce_fusion
  652.3 2.0 copy.92
  654.3 4.3 all-to-all-start.4
  658.6 5.7 fusion.20
  664.4 4.9 fusion.2
  669.3 2.9 fusion.17
  672.1 3.2 fusion.14
  675.3 3.9 all-to-all-done.4
  679.2 4.4 reshape.151
  683.6 5.5 gather_fusion
  689.1 3.5 gather.7
  692.6 5.7 multiply_reduce_fusion.1
  698.2 0.9 fusion.43
  (60 shorter events, 5.1 us)
Async XLA Ops:
  7.2 467.8 %copy-start = (bf16[256,2048]{1,0:T(8,128)(2,1)S(1)}, bf16[256,2048]{1,0:T(8,128)(2,1)}, u32[]{:S(2)}) copy-start(bf16[256,2048]{1,0:T(8,128)(2,1)} %param.24) | copy-start | bytes 3145732
  9.8 6.4 copy-start.5
  9.8 37.3 %all-to-all-start = ((bf16[8,128,1024]{2,1,0:T(8,128)(2,1)}), bf16[8,128,1024]{2,1,0:T(8,128)(2,1)S(1)}, u32[]{:S(2)}, u32[]{:S(2)}) async-start(bf16[8,128,1024]{2,1,0:T(8,128)(2,1)} %stack.3), calls=%async_computation | async-start | bytes 4194304 | tf_op jit(solution)/shard_map/all_to_all | solution.py:37
  15.5 49.0 %all-gather.3.cloned.1.call-start = ((), (), s32[]{:S(2)}) async-start(), calls=%async_computation.5 | async-start | bytes 2359296 | tf_op jit(solution)/shard_map/all_gather | solution.py:39
  22.7 6.0 copy-start.7
  48.6 1.9 copy-start.1
  67.4 3.5 copy-start.3
  67.4 3.6 copy-start.4
  71.0 0.8 copy-start.6
  444.2 20.7 %copy-start.9 = (bf16[256,2048]{1,0:T(8,128)(2,1)S(1)}, bf16[256,2048]{1,0:T(8,128)(2,1)}, u32[]{:S(2)}) copy-start(bf16[256,2048]{1,0:T(8,128)(2,1)} %param.22) | copy-start | bytes 3145732
  465.0 6.4 copy-start.2
  465.0 6.6 copy-start.10
  471.6 3.4 copy-start.11
  500.8 7.9 %copy-start.8 = (f32[1,128,2]{1,2,0:T(2,128)S(1)}, f32[1,128,2]{1,2,0:T(2,128)}, u32[]{:S(2)}) copy-start(f32[1,128,2]{1,2,0:T(2,128)} %param.21) | copy-start | bytes 3076
  500.8 147.8 %all-to-all-start.3 = ((bf16[8,32,12288]{2,0,1:T(8,128)(2,1)}), bf16[8,32,12288]{2,0,1:T(8,128)(2,1)}, u32[]{:S(2)}, u32[]{:S(2)}) async-start(bf16[8,32,12288]{2,0,1:T(8,128)(2,1)} %copy.91), calls=%async_computation.3 | async-start | bytes 12582912 | tf_op jit(solution)/shard_map/all_to_all | solution.py:110
  654.3 24.9 %all-to-all-start.4 = ((bf16[8,8,12288]{2,1,0:T(8,128)(2,1)}), bf16[8,8,12288]{2,1,0:T(8,128)(2,1)}, u32[]{:S(2)}, u32[]{:S(2)}) async-start(bf16[8,8,12288]{2,1,0:T(8,128)(2,1)} %copy.92), calls=%async_computation.4 | async-start | bytes 3145728 | tf_op jit(solution)/shard_map/all_to_all | solution.py:114
  658.6 10.6 %slice-start = ((s8[12582912]{0:T(1024)(128)(4,1)}), s8[4194304]{0:T(1024)(128)(4,1)S(1)}, s32[]{:S(2)}) async-start(s8[12582912]{0:T(1024)(128)(4,1)} %bitcast.65), calls=%async_computation.6 | async-start | bytes 8388608
  658.6 10.6 %slice-start.1 = ((s8[12582912]{0:T(1024)(128)(4,1)}), s8[4194304]{0:T(1024)(128)(4,1)S(1)}, s32[]{:S(2)}) async-start(s8[12582912]{0:T(1024)(128)(4,1)} %bitcast.65), calls=%async_computation.7 | async-start | bytes 8388608
  664.3 4.9 slice-start.2
  664.3 4.9 copy-start.12
  669.3 2.9 copy-start.13
Sparse Core Ops, SparseCore 0:
  18.1 46.4 all-gather.2
